TPU v7x, 32 devices: a whole 2x2x4 slice. The times are simulated.
32 devices in a mesh: row: 8 (over z, x), col: 4 (over y, core).
Axes of the slice: x: 2, y: 2, z: 4, core: 2. Of those that a mesh axis runs over, the one named last changes fastest.
Arguments:
- block_cost: bfloat16 [128, 16, 256, 256], P('row', 'col'), may hold values from 0 to 15, as said below
- candidates: int32 [128, 16], P('row', 'col'), may hold values from 0 to 31, all different within a row
- source_logmass: float32 [128, 256], P('row'), may hold values from -4 to 4
- target_logmass: float32 [32, 256], replicated, may hold values from -4 to 4
Outputs:
- source_potential: float32 [128, 256], P('row')
- target_potential: float32 [32, 256], replicated
Inputs may be any that keep to these rules, and one draw needn't show every extreme that they name: Each row of candidates names 16 distinct target blocks, and every target block is named by some row. `block_cost`: costs are nonnegative.
All inputs are finite; a program needn't handle non-finite values.
Results may differ from a plain program's by a relative error of at most 0.0003.
Values sent between devices are 32-bit elements; how exact they have to be, the bound alone decides.
No kernel may reach another device: no remote copies, remote signals or barrier semaphores. Data moves between devices by JAX's collectives and lax.ppermute only.
A program may use at most 256 MiB of HBM per device.

v0:
```python
import jax
import jax.numpy as jnp
from jax import lax
from jax.sharding import PartitionSpec as P

ITERS = 2
EPS = 0.05
LOWEST = -1e30


def per_device(block_cost, candidates, source_logmass, target_logmass):
    target_pot = jnp.zeros(target_logmass.shape, jnp.float32)
    source_pot = jnp.zeros(source_logmass.shape, jnp.float32)
    block_size = block_cost.shape[3]
    flat_ids = candidates.reshape(-1)
    for step_index in range(ITERS):
        nearby = target_pot[candidates]
        scores = (nearby[:, :, None, :] - block_cost.astype(jnp.float32)) / EPS
        highest = jnp.max(scores, axis=(1, 3))
        totals = jnp.sum(jnp.exp(scores - highest[:, None, :, None]), axis=(1, 3))
        row_peak = lax.pmax(highest, "col")
        totals = lax.psum(totals * jnp.exp(highest - row_peak), "col")
        highest = row_peak
        source_pot = EPS * source_logmass - EPS * (highest + jnp.log(totals))
        col_scores = (source_pot[:, None, :, None] - block_cost.astype(jnp.float32)) / EPS
        col_high = jnp.max(col_scores, axis=2).reshape(-1, block_size)
        col_total = jnp.sum(
            jnp.exp(col_scores - jnp.max(col_scores, axis=2)[:, :, None, :]), axis=2
        ).reshape(-1, block_size)
        peaks = jnp.full(target_logmass.shape, LOWEST, jnp.float32).at[flat_ids].max(col_high)
        masses = (
            jnp.zeros(target_logmass.shape, jnp.float32)
            .at[flat_ids]
            .add(col_total * jnp.exp(col_high - peaks[flat_ids]))
        )
        all_peaks = lax.pmax(peaks, ("row", "col"))
        masses = lax.psum(masses * jnp.exp(peaks - all_peaks), ("row", "col"))
        target_pot = EPS * target_logmass - EPS * (all_peaks + jnp.log(masses))
    return (source_pot, target_pot)


def solution(mesh):
    return jax.shard_map(
        per_device,
        mesh=mesh,
        in_specs=(P("row", "col", None, None), P("row", "col"), P("row", None), P()),
        out_specs=(P("row", None), P()),
        check_vma=False,
    )
```

profile of v0, /device:TPU:0, one launch (start us, length us, event | category | flops | bytes accessed | tf_op | source)
XLA Modules:
  0.0 260.1 jit_solution(773136347404599062)
XLA Ops:
  0.6 0.7 compare_select_fusion
  1.3 0.1 copy.9
  1.4 0.1 reshape.62
  1.5 0.8 copy.8
  2.3 0.1 reshape.55
  2.4 0.7 gather_fusion
  3.1 0.0 copy-start
  3.1 0.0 copy-start.3
  3.1 5.8 %fusion.2 = f32[16,256]{1,0:T(8,128)S(1)} fusion(bf16[16,4,256,256]{3,2,1,0:T(8,128)(2,1)} %param.4, f32[16,4,256]{2,1,0:T(4,128)S(1)} %reshape.61), kind=kLoop, calls=%fused_computation.14 | loop fusion | flops 16773120 | bytes 8470528 | tf_op jit(solution)/shard_map/reduce_max | solution.py:19
  8.9 0.0 copy-done
  8.9 4.6 %fusion.4 = f32[16,256]{1,0:T(8,128)S(1)} fusion(bf16[16,4,256,256]{3,2,1,0:T(8,128)(2,1)S(1)} %copy-done, f32[16,256]{1,0:T(8,128)S(1)} %fusion.2, f32[16,4,256]{2,1,0:T(4,128)S(1)} %reshape.61), kind=kLoop, calls=%fused_computation.16 | loop fusion | flops 20967424 | bytes 8486912 | tf_op jit(solution)/shard_map/reduce_sum | solution.py:20
  13.6 12.7 %pmax.28 = f32[16,256]{1,0:T(8,128)S(1)} all-reduce(f32[16,256]{1,0:T(8,128)S(1)} %fusion.2), channel_id=1, replica_groups=mesh['row'=8,'col'=4] {'col'}, use_global_device_ids=true, to_apply=%region_1.0 | all-reduce | flops 4096 | bytes 32768 | tf_op jit(solution)/shard_map/pmax | solution.py:21
  26.3 10.1 %psum.28 = f32[16,256]{1,0:T(8,128)S(1)} all-reduce(f32[16,256]{1,0:T(8,128)S(1)} %exponential_multiply_fusion.3), channel_id=1, replica_groups=mesh['row'=8,'col'=4] {'col'}, use_global_device_ids=true, to_apply=%region_3.0 | all-reduce | flops 4096 | bytes 32768 | tf_op jit(solution)/shard_map/psum | solution.py:22
  36.4 0.0 copy-done.3
  36.4 0.0 copy-start.2
  36.4 5.3 %fusion.7 = f32[16,4,256]{2,1,0:T(4,128)S(1)} fusion(bf16[16,4,256,256]{3,2,1,0:T(8,128)(2,1)} %param.4, f32[16,256]{1,0:T(8,128)S(1)} %multiply_subtract_fusion.3), kind=kLoop, calls=%fused_computation.19 | loop fusion | flops 16760832 | bytes 8470528 | tf_op jit(solution)/shard_map/reduce_max | solution.py:26
  41.7 6.6 %fusion.9 = f32[16,4,256]{2,1,0:T(4,128)S(1)} fusion(bf16[16,4,256,256]{3,2,1,0:T(8,128)(2,1)} %param.4, f32[16,4,256]{2,1,0:T(4,128)S(1)} %fusion.7, f32[16,256]{1,0:T(8,128)S(1)} %multiply_subtract_fusion.3), kind=kLoop, calls=%fused_computation.21 | loop fusion | flops 20955136 | bytes 8536064 | tf_op jit(solution)/shard_map/reduce_sum | solution.py:27
  48.4 0.9 scatter_custom_fusion
  49.4 1.1 scatter_custom_fusion.1
  50.5 39.7 %pmax.29 = f32[32,256]{1,0:T(8,128)S(1)} all-reduce(f32[32,256]{1,0:T(8,128)S(1)} %scatter_custom_fusion), channel_id=1, replica_groups=mesh['row'=8,'col'=4] {'row','col'}, use_global_device_ids=true, to_apply=%region_6.0 | all-reduce | flops 8192 | bytes 65536 | tf_op jit(solution)/shard_map/pmax | solution.py:36
  90.3 41.3 %psum.29 = f32[32,256]{1,0:T(8,128)S(1)} all-reduce(f32[32,256]{1,0:T(8,128)S(1)} %exponential_multiply_fusion.1), channel_id=1, replica_groups=mesh['row'=8,'col'=4] {'row','col'}, use_global_device_ids=true, to_apply=%region_9.0 | all-reduce | flops 8192 | bytes 65536 | tf_op jit(solution)/shard_map/psum | solution.py:37
  131.5 0.0 copy-done.2
  131.6 0.7 gather_fusion.1
  132.3 5.7 %fusion.12 = f32[16,256]{1,0:T(8,128)S(1)} fusion(bf16[16,4,256,256]{3,2,1,0:T(8,128)(2,1)} %param.4, f32[16,4,256]{2,1,0:T(4,128)S(1)} %reshape.77), kind=kLoop, calls=%fused_computation.24 | loop fusion | flops 16773120 | bytes 8470528 | tf_op jit(solution)/shard_map/reduce_max | solution.py:19
  137.9 6.7 %fusion.14 = f32[16,256]{1,0:T(8,128)S(1)} fusion(bf16[16,4,256,256]{3,2,1,0:T(8,128)(2,1)} %param.4, f32[16,256]{1,0:T(8,128)S(1)} %fusion.12, f32[16,4,256]{2,1,0:T(4,128)S(1)} %reshape.77), kind=kLoop, calls=%fused_computation.26 | loop fusion | flops 20967424 | bytes 8486912 | tf_op jit(solution)/shard_map/reduce_sum | solution.py:20
  144.6 10.2 %pmax.30 = f32[16,256]{1,0:T(8,128)S(1)} all-reduce(f32[16,256]{1,0:T(8,128)S(1)} %fusion.12), channel_id=1, replica_groups=mesh['row'=8,'col'=4] {'col'}, use_global_device_ids=true, to_apply=%region_11.0 | all-reduce | flops 4096 | bytes 32768 | tf_op jit(solution)/shard_map/pmax | solution.py:21
  154.8 10.1 %psum.30 = f32[16,256]{1,0:T(8,128)S(1)} all-reduce(f32[16,256]{1,0:T(8,128)S(1)} %exponential_multiply_fusion.2), channel_id=1, replica_groups=mesh['row'=8,'col'=4] {'col'}, use_global_device_ids=true, to_apply=%region_13.0 | all-reduce | flops 4096 | bytes 32768 | tf_op jit(solution)/shard_map/psum | solution.py:22
  164.9 0.0 copy-start.1
  164.9 5.3 %fusion.17 = f32[16,4,256]{2,1,0:T(4,128)S(1)} fusion(bf16[16,4,256,256]{3,2,1,0:T(8,128)(2,1)} %param.4, f32[16,256]{1,0:T(8,128)S(1)} %multiply_subtract_fusion.2), kind=kLoop, calls=%fused_computation.29 | loop fusion | flops 16760832 | bytes 8470528 | tf_op jit(solution)/shard_map/reduce_max | solution.py:26
  170.3 6.6 %fusion.19 = f32[16,4,256]{2,1,0:T(4,128)S(1)} fusion(bf16[16,4,256,256]{3,2,1,0:T(8,128)(2,1)} %param.4, f32[16,4,256]{2,1,0:T(4,128)S(1)} %fusion.17, f32[16,256]{1,0:T(8,128)S(1)} %multiply_subtract_fusion.2), kind=kLoop, calls=%fused_computation.31 | loop fusion | flops 20955136 | bytes 8536064 | tf_op jit(solution)/shard_map/reduce_sum | solution.py:27
  176.9 0.0 copy-done.1
  176.9 0.9 scatter_custom_fusion.2
  177.9 1.1 scatter_custom_fusion.3
  179.0 39.2 %pmax.31 = f32[32,256]{1,0:T(8,128)S(1)} all-reduce(f32[32,256]{1,0:T(8,128)S(1)} %scatter_custom_fusion.2), channel_id=1, replica_groups=mesh['row'=8,'col'=4] {'row','col'}, use_global_device_ids=true, to_apply=%region_16.0 | all-reduce | flops 8192 | bytes 65536 | tf_op jit(solution)/shard_map/pmax | solution.py:36
  218.2 41.2 %psum.31 = f32[32,256]{1,0:T(8,128)S(1)} all-reduce(f32[32,256]{1,0:T(8,128)S(1)} %exponential_multiply_fusion), channel_id=1, replica_groups=mesh['row'=8,'col'=4] {'row','col'}, use_global_device_ids=true, to_apply=%region_19.0 | all-reduce | flops 8192 | bytes 65536 | tf_op jit(solution)/shard_map/psum | solution.py:37
  259.5 0.6 multiply_subtract_fusion
  (17 shorter events, 0.3 us)
Async XLA Ops:
  3.1 5.8 %copy-start = (bf16[16,4,256,256]{3,2,1,0:T(8,128)(2,1)S(1)}, bf16[16,4,256,256]{3,2,1,0:T(8,128)(2,1)}, u32[]{:S(2)}) copy-start(bf16[16,4,256,256]{3,2,1,0:T(8,128)(2,1)} %param.4) | copy-start | bytes 25165828
  3.1 33.3 %copy-start.3 = (f32[16,256]{1,0:T(8,128)S(1)}, f32[16,256]{1,0:T(8,128)}, u32[]{:S(2)}) copy-start(f32[16,256]{1,0:T(8,128)} %param.6) | copy-start | bytes 49156
  36.4 95.1 %copy-start.2 = (f32[32,256]{1,0:T(8,128)S(1)}, f32[32,256]{1,0:T(8,128)}, u32[]{:S(2)}) copy-start(f32[32,256]{1,0:T(8,128)} %param.7) | copy-start | bytes 98308
  164.9 12.0 %copy-start.1 = (f32[16,256]{1,0:T(8,128)}, f32[16,256]{1,0:T(8,128)S(1)}, u32[]{:S(2)}) copy-start(f32[16,256]{1,0:T(8,128)S(1)} %multiply_subtract_fusion.2) | copy-start | bytes 49156
where the time goes:
time: 261 us; the launch traced here: 260 us
  blocking collectives  204 us (78%)
  other arithmetic  52.2 us (20%)
    psum x2, blocking collectives, per_device(): masses = lax.psum(masses * jnp.exp(peaks - all_peaks), ('row', 'col'))  82.5 us
    pmax x2, blocking collectives, per_device(): all_peaks = lax.pmax(peaks, ('row', 'col'))  78.9 us
    pmax x2, blocking collectives, per_device(): row_peak = lax.pmax(highest, 'col')  22.9 us
    psum x2, blocking collectives, per_device(): totals = lax.psum(totals * jnp.exp(highest - row_peak), 'col')  20.2 us
    reduce_sum x2, other arithmetic, per_device(): jnp.sum(jnp.exp(col_scores - jnp.max(col_scores, axis=2)[:, :, None, :]),...  13.2 us
    reduce_max x2, other arithmetic, per_device(): highest = jnp.max(scores, axis=(1, 3))  11.5 us
    reduce_sum x2, other arithmetic, per_device(): totals = jnp.sum(jnp.exp(scores - highest[:, None, :, None]), axis=(1, 3))  11.3 us
    reduce_max x2, other arithmetic, per_device(): col_high = jnp.max(col_scores, axis=2).reshape(-1, block_size)  10.6 us

commit v1 on v0

--- a/solution.py
+++ b/solution.py
@@ -34,7 +34,8 @@
             .add(col_total * jnp.exp(col_high - peaks[flat_ids]))
         )
         all_peaks = lax.pmax(peaks, ("row", "col"))
-        masses = lax.psum(masses * jnp.exp(peaks - all_peaks), ("row", "col"))
+        partial = lax.psum(masses * jnp.exp(peaks - all_peaks), "col")
+        masses = lax.psum(partial, "row")
         target_pot = EPS * target_logmass - EPS * (all_peaks + jnp.log(masses))
     return (source_pot, target_pot)
 

time: 261 us -> 270 us (1.034)
  blocking collectives: 204 us -> 214 us
    psum x2 -> x4, blocking collectives: 82.5 us -> 94.2 us  [the longest x2 71.8 us: per_device(): masses = lax.psum(partial, 'row')]
where the time goes in v1:
time: 270 us
  blocking collectives  214 us (79%)
  other arithmetic  52.2 us (19%)
    pmax x2, blocking collectives, per_device(): all_peaks = lax.pmax(peaks, ('row', 'col'))  76.8 us
    psum x2, blocking collectives, per_device(): masses = lax.psum(partial, 'row')  71.8 us
    pmax x2, blocking collectives, per_device(): row_peak = lax.pmax(highest, 'col')  22.8 us
    psum x2, blocking collectives, per_device(): partial = lax.psum(masses * jnp.exp(peaks - all_peaks), 'col')  22.4 us
    psum x2, blocking collectives, per_device(): totals = lax.psum(totals * jnp.exp(highest - row_peak), 'col')  20.2 us
    reduce_sum x2, other arithmetic, per_device(): jnp.sum(jnp.exp(col_scores - jnp.max(col_scores, axis=2)[:, :, None, :]),...  13.2 us
    reduce_max x2, other arithmetic, per_device(): highest = jnp.max(scores, axis=(1, 3))  11.5 us
    reduce_sum x2, other arithmetic, per_device(): totals = jnp.sum(jnp.exp(scores - highest[:, None, :, None]), axis=(1, 3))  11.3 us

profile of v1, /device:TPU:0, one launch (start us, length us, event | category | flops | bytes accessed | tf_op | source)
XLA Modules:
  0.0 269.6 jit_solution(13488842983107419989)
XLA Ops:
  0.6 0.7 compare_select_fusion
  1.3 0.1 copy.9
  1.4 0.1 reshape.62
  1.5 0.8 copy.8
  2.3 0.1 reshape.55
  2.4 0.7 gather_fusion
  3.1 0.0 copy-start
  3.1 0.0 copy-start.3
  3.1 5.8 %fusion.2 = f32[16,256]{1,0:T(8,128)S(1)} fusion(bf16[16,4,256,256]{3,2,1,0:T(8,128)(2,1)} %param.4, f32[16,4,256]{2,1,0:T(4,128)S(1)} %reshape.61), kind=kLoop, calls=%fused_computation.14 | loop fusion | flops 16773120 | bytes 8470528 | tf_op jit(solution)/shard_map/reduce_max | solution.py:19
  8.9 0.0 copy-done
  8.9 4.6 %fusion.4 = f32[16,256]{1,0:T(8,128)S(1)} fusion(bf16[16,4,256,256]{3,2,1,0:T(8,128)(2,1)S(1)} %copy-done, f32[16,256]{1,0:T(8,128)S(1)} %fusion.2, f32[16,4,256]{2,1,0:T(4,128)S(1)} %reshape.61), kind=kLoop, calls=%fused_computation.16 | loop fusion | flops 20967424 | bytes 8486912 | tf_op jit(solution)/shard_map/reduce_sum | solution.py:20
  13.6 12.7 %pmax.28 = f32[16,256]{1,0:T(8,128)S(1)} all-reduce(f32[16,256]{1,0:T(8,128)S(1)} %fusion.2), channel_id=1, replica_groups=mesh['row'=8,'col'=4] {'col'}, use_global_device_ids=true, to_apply=%region_1.0 | all-reduce | flops 4096 | bytes 32768 | tf_op jit(solution)/shard_map/pmax | solution.py:21
  26.3 10.1 %psum.42 = f32[16,256]{1,0:T(8,128)S(1)} all-reduce(f32[16,256]{1,0:T(8,128)S(1)} %exponential_multiply_fusion.3), channel_id=1, replica_groups=mesh['row'=8,'col'=4] {'col'}, use_global_device_ids=true, to_apply=%region_3.0 | all-reduce | flops 4096 | bytes 32768 | tf_op jit(solution)/shard_map/psum | solution.py:22
  36.4 0.0 copy-done.3
  36.4 0.0 copy-start.2
  36.4 5.3 %fusion.7 = f32[16,4,256]{2,1,0:T(4,128)S(1)} fusion(bf16[16,4,256,256]{3,2,1,0:T(8,128)(2,1)} %param.4, f32[16,256]{1,0:T(8,128)S(1)} %multiply_subtract_fusion.3), kind=kLoop, calls=%fused_computation.19 | loop fusion | flops 16760832 | bytes 8470528 | tf_op jit(solution)/shard_map/reduce_max | solution.py:26
  41.7 6.6 %fusion.9 = f32[16,4,256]{2,1,0:T(4,128)S(1)} fusion(bf16[16,4,256,256]{3,2,1,0:T(8,128)(2,1)} %param.4, f32[16,4,256]{2,1,0:T(4,128)S(1)} %fusion.7, f32[16,256]{1,0:T(8,128)S(1)} %multiply_subtract_fusion.3), kind=kLoop, calls=%fused_computation.21 | loop fusion | flops 20955136 | bytes 8536064 | tf_op jit(solution)/shard_map/reduce_sum | solution.py:27
  48.4 0.9 scatter_custom_fusion
  49.4 1.1 scatter_custom_fusion.1
  50.5 39.7 %pmax.29 = f32[32,256]{1,0:T(8,128)S(1)} all-reduce(f32[32,256]{1,0:T(8,128)S(1)} %scatter_custom_fusion), channel_id=1, replica_groups=mesh['row'=8,'col'=4] {'row','col'}, use_global_device_ids=true, to_apply=%region_6.0 | all-reduce | flops 8192 | bytes 65536 | tf_op jit(solution)/shard_map/pmax | solution.py:36
  90.3 11.2 %psum.43 = f32[32,256]{1,0:T(8,128)S(1)} all-reduce(f32[32,256]{1,0:T(8,128)S(1)} %exponential_multiply_fusion.1), channel_id=1, replica_groups=mesh['row'=8,'col'=4] {'col'}, use_global_device_ids=true, to_apply=%region_9.0 | all-reduce | flops 8192 | bytes 65536 | tf_op jit(solution)/shard_map/psum | solution.py:37
  101.5 35.9 %psum.44 = f32[32,256]{1,0:T(8,128)S(1)} all-reduce(f32[32,256]{1,0:T(8,128)S(1)} %psum.43), channel_id=1, replica_groups=mesh['row'=8,'col'=4] {'row'}, use_global_device_ids=true, to_apply=%region_10.0 | all-reduce | flops 8192 | bytes 65536 | tf_op jit(solution)/shard_map/psum | solution.py:38
  137.3 0.0 copy-done.2
  137.3 0.7 gather_fusion.1
  138.0 5.7 %fusion.12 = f32[16,256]{1,0:T(8,128)S(1)} fusion(bf16[16,4,256,256]{3,2,1,0:T(8,128)(2,1)} %param.4, f32[16,4,256]{2,1,0:T(4,128)S(1)} %reshape.77), kind=kLoop, calls=%fused_computation.24 | loop fusion | flops 16773120 | bytes 8470528 | tf_op jit(solution)/shard_map/reduce_max | solution.py:19
  143.7 6.7 %fusion.14 = f32[16,256]{1,0:T(8,128)S(1)} fusion(bf16[16,4,256,256]{3,2,1,0:T(8,128)(2,1)} %param.4, f32[16,256]{1,0:T(8,128)S(1)} %fusion.12, f32[16,4,256]{2,1,0:T(4,128)S(1)} %reshape.77), kind=kLoop, calls=%fused_computation.26 | loop fusion | flops 20967424 | bytes 8486912 | tf_op jit(solution)/shard_map/reduce_sum | solution.py:20
  150.4 10.1 %pmax.30 = f32[16,256]{1,0:T(8,128)S(1)} all-reduce(f32[16,256]{1,0:T(8,128)S(1)} %fusion.12), channel_id=1, replica_groups=mesh['row'=8,'col'=4] {'col'}, use_global_device_ids=true, to_apply=%region_12.0 | all-reduce | flops 4096 | bytes 32768 | tf_op jit(solution)/shard_map/pmax | solution.py:21
  160.5 10.1 %psum.45 = f32[16,256]{1,0:T(8,128)S(1)} all-reduce(f32[16,256]{1,0:T(8,128)S(1)} %exponential_multiply_fusion.2), channel_id=1, replica_groups=mesh['row'=8,'col'=4] {'col'}, use_global_device_ids=true, to_apply=%region_14.0 | all-reduce | flops 4096 | bytes 32768 | tf_op jit(solution)/shard_map/psum | solution.py:22
  170.6 0.0 copy-start.1
  170.6 5.3 %fusion.17 = f32[16,4,256]{2,1,0:T(4,128)S(1)} fusion(bf16[16,4,256,256]{3,2,1,0:T(8,128)(2,1)} %param.4, f32[16,256]{1,0:T(8,128)S(1)} %multiply_subtract_fusion.2), kind=kLoop, calls=%fused_computation.29 | loop fusion | flops 16760832 | bytes 8470528 | tf_op jit(solution)/shard_map/reduce_max | solution.py:26
  176.0 6.6 %fusion.19 = f32[16,4,256]{2,1,0:T(4,128)S(1)} fusion(bf16[16,4,256,256]{3,2,1,0:T(8,128)(2,1)} %param.4, f32[16,4,256]{2,1,0:T(4,128)S(1)} %fusion.17, f32[16,256]{1,0:T(8,128)S(1)} %multiply_subtract_fusion.2), kind=kLoop, calls=%fused_computation.31 | loop fusion | flops 20955136 | bytes 8536064 | tf_op jit(solution)/shard_map/reduce_sum | solution.py:27
  182.6 0.0 copy-done.1
  182.7 0.9 scatter_custom_fusion.2
  183.6 1.1 scatter_custom_fusion.3
  184.7 37.1 %pmax.31 = f32[32,256]{1,0:T(8,128)S(1)} all-reduce(f32[32,256]{1,0:T(8,128)S(1)} %scatter_custom_fusion.2), channel_id=1, replica_groups=mesh['row'=8,'col'=4] {'row','col'}, use_global_device_ids=true, to_apply=%region_17.0 | all-reduce | flops 8192 | bytes 65536 | tf_op jit(solution)/shard_map/pmax | solution.py:36
  221.8 11.2 %psum.46 = f32[32,256]{1,0:T(8,128)S(1)} all-reduce(f32[32,256]{1,0:T(8,128)S(1)} %exponential_multiply_fusion), channel_id=1, replica_groups=mesh['row'=8,'col'=4] {'col'}, use_global_device_ids=true, to_apply=%region_20.0 | all-reduce | flops 8192 | bytes 65536 | tf_op jit(solution)/shard_map/psum | solution.py:37
  233.0 35.9 %psum.47 = f32[32,256]{1,0:T(8,128)S(1)} all-reduce(f32[32,256]{1,0:T(8,128)S(1)} %psum.46), channel_id=1, replica_groups=mesh['row'=8,'col'=4] {'row'}, use_global_device_ids=true, to_apply=%region_21.0 | all-reduce | flops 8192 | bytes 65536 | tf_op jit(solution)/shard_map/psum | solution.py:38
  269.0 0.6 multiply_subtract_fusion
  (17 shorter events, 0.3 us)
Async XLA Ops:
  3.1 5.8 %copy-start = (bf16[16,4,256,256]{3,2,1,0:T(8,128)(2,1)S(1)}, bf16[16,4,256,256]{3,2,1,0:T(8,128)(2,1)}, u32[]{:S(2)}) copy-start(bf16[16,4,256,256]{3,2,1,0:T(8,128)(2,1)} %param.4) | copy-start | bytes 25165828
  3.1 33.3 %copy-start.3 = (f32[16,256]{1,0:T(8,128)S(1)}, f32[16,256]{1,0:T(8,128)}, u32[]{:S(2)}) copy-start(f32[16,256]{1,0:T(8,128)} %param.6) | copy-start | bytes 49156
  36.4 100.9 %copy-start.2 = (f32[32,256]{1,0:T(8,128)S(1)}, f32[32,256]{1,0:T(8,128)}, u32[]{:S(2)}) copy-start(f32[32,256]{1,0:T(8,128)} %param.7) | copy-start | bytes 98308
  170.6 12.0 %copy-start.1 = (f32[16,256]{1,0:T(8,128)}, f32[16,256]{1,0:T(8,128)S(1)}, u32[]{:S(2)}) copy-start(f32[16,256]{1,0:T(8,128)S(1)} %multiply_subtract_fusion.2) | copy-start | bytes 49156
